TPU v7x, 256 devices: a whole 4x4x8 slice. The times are simulated.
256 devices in a mesh: dp: 4 (over x), cls: 64 (over z, y, core).
Axes of the slice: x: 4, y: 4, z: 8, core: 2. Of those that a mesh axis runs over, the one named last changes fastest.
Arguments:
- embeddings: float32 [2048, 512], P('dp'), may hold values from -60 to 60, as said below
- classifier: float32 [1048576, 512], P(('dp', 'cls')), may hold values from -60 to 60, as said below
- labels: int32 [2048], replicated, may hold values from 0 to 1048575
- row_scale: float32 [2048], replicated, may hold values from 16 to 512
Outputs:
- loss: float32 [2048], P(('dp', 'cls'))
Inputs may be any that keep to these rules, and one draw needn't show every extreme that they name: `embeddings`: rows of different scales. `classifier`: rows of different scales.
All inputs are finite; a program needn't handle non-finite values.
Results may differ from a plain program's by a relative error of at most 0.0003.
Values sent between devices are 32-bit elements; how exact they have to be, the bound alone decides.
No kernel may reach another device: no remote copies, remote signals or barrier semaphores. Data moves between devices by JAX's collectives and lax.ppermute only.
A program may use at most 128 MiB of HBM per device.

v0:
```python
import math

import jax
import jax.numpy as jnp
from jax import lax
from jax.sharding import Mesh
from jax.sharding import PartitionSpec as P

DP_CLS = ("dp", "cls_0", "cls_1", "cls_2")


MARGIN = 0.5
COS_MARGIN = math.cos(MARGIN)
SIN_MARGIN = math.sin(MARGIN)


def gathered_once(shard, axis):
    leaves = jax.tree.leaves(shard)
    sequence = sorted(range(len(leaves)), key=lambda k: -leaves[k].size)
    width = (1, *leaves[sequence[0]].shape)[-1]
    lines = [
        jnp.pad(leaves[k].reshape(-1), (0, -leaves[k].size % width)).reshape(-1, width)
        for k in sequence
    ]
    both, at, found = (lax.all_gather(jnp.concatenate(lines), axis), 0, {})
    for k, line in zip(sequence, lines):
        section = both[:, at : at + len(line)].reshape(len(both), -1)
        found[k] = section[:, : leaves[k].size].reshape(-1, *leaves[k].shape)
        at += len(line)
    numbers = iter(range(len(leaves)))
    return jax.tree.map(lambda _: found[next(numbers)], shard)


def merged_by_axis(shard, axes, combine):
    for axis in axes:
        pieces = gathered_once(shard, axis)
        shard = jax.tree.map(lambda part: part[0], pieces)
        for k in range(1, lax.axis_size(axis)):
            shard = combine(shard, jax.tree.map(lambda part: part[k], pieces))
    return shard


def unit_rows(values):
    return values * lax.rsqrt(jnp.sum(values * values, axis=-1, keepdims=True) + 1e-06)


def margin_logit(units, picked, scales):
    cosine = jnp.sum(units * picked, axis=-1)
    across = units - cosine[:, None] * picked
    sine = jnp.sqrt(jnp.sum(across * across, axis=-1))
    return scales * (cosine * COS_MARGIN - sine * SIN_MARGIN)


def block_stats(units, rows, class_ids, labels, scales, picked, owned):
    cosine = lax.dot_general(
        units,
        rows,
        (((1,), (1,)), ((), ())),
        precision=lax.Precision.HIGHEST,
        preferred_element_type=jnp.float32,
    )
    target = margin_logit(units, picked, scales)
    hit = labels[:, None] == class_ids[None, :]
    logits = jnp.where(hit, target[:, None], scales[:, None] * cosine)
    peak = jnp.max(logits, axis=1)
    total = jnp.sum(jnp.exp(logits - peak[:, None]), axis=1)
    return (peak, total, jnp.where(owned, target, jnp.zeros_like(target)))


def merge_rows(first, second):
    peak = jnp.maximum(first[0], second[0])
    total = first[1] * jnp.exp(first[0] - peak) + second[1] * jnp.exp(second[0] - peak)
    return (peak, total, first[2] + second[2])


def body(embeddings, classifier, labels, row_scale):
    rows_here = classifier.shape[0]
    units_mine = unit_rows(embeddings)
    normed = unit_rows(classifier)
    offset = lax.axis_index(DP_CLS) * rows_here
    class_ids = offset + jnp.arange(rows_here, dtype=jnp.int32)
    owned_all = (labels >= offset) & (labels < offset + rows_here)
    local_all = jnp.clip(labels - offset, 0, rows_here - 1)
    count = labels.shape[0]
    picked = jnp.take(normed, local_all, axis=0)
    stats = block_stats(
        lax.all_gather(units_mine, "dp", axis=0, tiled=True),
        normed,
        class_ids,
        labels,
        row_scale,
        picked,
        owned_all,
    )
    peak, total, target = tuple((fresh for fresh in stats))
    share = count // lax.axis_size(DP_CLS)
    first = lax.axis_index(DP_CLS) * share
    peak, total, target = merged_by_axis((peak, total, target), DP_CLS, merge_rows)
    whole = peak + jnp.log(total) - target
    return lax.dynamic_slice_in_dim(whole, first, share)


def solution(mesh):
    torus = Mesh(mesh.devices.reshape(mesh.shape["dp"], 8, 4, 2), ("dp", "cls_0", "cls_1", "cls_2"))
    return jax.shard_map(
        body,
        mesh=torus,
        in_specs=(P("dp", None), P(DP_CLS, None), P(), P()),
        out_specs=P(DP_CLS),
        check_vma=False,
    )
```

profile of v0, /device:TPU:1, one launch (start us, length us, event | category | flops | bytes accessed | tf_op | source)
XLA Modules:
  0.0 210.5 jit_solution(7871280436764989805)
XLA Ops:
  6.5 0.0 all-gather.10.cloned.1.call-start
  6.5 1.4 multiply_reduce_fusion.3
  7.9 2.3 %broadcast_multiply_fusion.1 = f32[512,512]{1,0:T(8,128)} fusion(f32[512,512]{1,0:T(8,128)} %param.4, f32[512]{0:T(512)S(1)} %add_rsqrt_fusion.1), kind=kLoop, calls=%fused_computation.9 | loop fusion | flops 262144 | bytes 2099200 | tf_op jit(solution)/shard_map/mul | solution.py:44
  10.3 0.0 all-gather.10.cloned.1.call-update
  10.3 0.0 copy-start.1
  10.3 0.9 fusion.43
  11.2 4.1 %multiply_reduce_fusion = f32[4096]{0:T(1024)S(1)} fusion(f32[4096,512]{1,0:T(8,128)} %param.5), kind=kLoop, calls=%fused_computation.4 | loop fusion | flops 4190208 | bytes 8404992 | tf_op jit(solution)/shard_map/reduce_sum | solution.py:44
  15.3 0.8 copy-done.1
  16.1 3.6 %broadcast_multiply_fusion = f32[4096,512]{1,0:T(8,128)} fusion(f32[4096,512]{1,0:T(8,128)S(1)} %copy-done.1, f32[4096]{0:T(1024)S(1)} %add_rsqrt_fusion), kind=kLoop, calls=%fused_computation.7 | loop fusion | flops 2097152 | bytes 16793600 | tf_op jit(solution)/shard_map/mul | solution.py:44
  19.6 0.0 copy-start.3
  19.6 12.9 %gather_fusion = f32[2048,512]{1,0:T(8,128)} fusion(f32[4096,512]{1,0:T(8,128)} %broadcast_multiply_fusion, s32[2048]{0:T(1024)S(1)} %fusion.43), kind=kCustom, calls=%fused_computation | custom fusion | bytes 8396800 | tf_op jit(solution)/shard_map/jit(_take)/gather | solution.py:85
  32.6 0.0 copy-done.3
  32.6 0.0 copy-start.4
  32.6 32.2 %all-gather.10.cloned.1.call-done = f32[2048,512]{1,0:T(8,128)} async-done(((f32[512,512]{1,0:T(8,128)}), f32[2048,512]{1,0:T(8,128)}) %all-gather.10.cloned.1.call-update) | async-done | bytes 4194320 | tf_op jit(solution)/shard_map/all_gather | solution.py:87
  64.8 0.0 copy-start
  64.8 0.0 slice-start
  64.8 0.0 copy-start.2
  64.8 4.1 %multiply_reduce_fusion.2 = f32[2048]{0:T(1024)S(1)} fusion(f32[2048,512]{1,0:T(8,128)} %all-gather.10.cloned.1.call-done, f32[2048,512]{1,0:T(8,128)} %gather_fusion, pred[2048]{0:T(1024)(128)(4,1)S(1)} %compare_and_fusion), kind=kLoop, calls=%fused_computation.6 | loop fusion | flops 3143680 | bytes 8398848 | tf_op jit(solution)/shard_map/reduce_sum | solution.py:48
  68.9 0.6 copy-done
  69.5 0.0 slice-start.1
  69.5 3.6 %multiply_reduce_fusion.1 = f32[2048]{0:T(1024)S(1)} fusion(f32[2048,512]{1,0:T(8,128)} %all-gather.10.cloned.1.call-done, f32[2048,512]{1,0:T(8,128)S(1)} %copy-done, f32[2048]{0:T(1024)S(1)} %multiply_reduce_fusion.2, pred[2048]{0:T(1024)(128)(4,1)S(1)} %compare_and_fusion), kind=kLoop, calls=%fused_computation.5 | loop fusion | flops 5240832 | bytes 8407040 | tf_op jit(solution)/shard_map/reduce_sum | solution.py:50
  73.1 0.0 copy-done.4
  73.1 0.0 slice-done
  73.1 0.1 copy-done.2
  73.2 1.4 slice-done.1
  74.7 59.6 %fusion = (f32[2048]{0:T(1024)S(1)}, f32[2048,4096]{1,0:T(8,128)}) fusion(f32[2048]{0:T(1024)S(1)} %copy-done.4, f32[2048]{0:T(1024)S(1)} %get-tuple-element.14, s32[4096]{0:T(1024)S(1)} %iota_add_fusion, s32[2048]{0:T(1024)S(1)} %copy-done.3, f32[2048,512]{1,0:T(8,128)S(1)} %copy-done.2, f32[4096,512]{1,0:T(8,128)S(1)} %bitcast.325), kind=kOutput, calls=%fused_computation.3 | convolution fusion | flops 51573161984 | bytes 46186496 | tf_op jit(solution)/shard_map/dot_general | solution.py:55
  134.3 15.2 %exponential_reduce_fusion = f32[2048]{0:T(1024)S(1)} fusion(f32[2048,4096]{1,0:T(8,128)} %get-tuple-element.21, f32[2048]{0:T(1024)S(1)} %get-tuple-element.20, f32[2048]{0:T(1024)S(1)} %copy-done.4, f32[2048]{0:T(1024)S(1)} %get-tuple-element.14, s32[4096]{0:T(1024)S(1)} %iota_add_fusion, s32[2048]{0:T(1024)S(1)} %copy-done.3), kind=kLoop, calls=%fused_computation.1 | loop fusion | flops 41940992 | bytes 33611776 | tf_op jit(solution)/shard_map/reduce_sum | solution.py:66
  149.5 9.1 %all-gather.4 = f32[4,3,2048]{2,1,0:T(4,128)S(1)} all-gather(f32[1,3,2048]{2,1,0:T(4,128)S(1)} %maximum_bitcast_fusion), channel_id=2, replica_groups=mesh['dp'=4,'cls_0'=8,'cls_1'=4,'cls_2'=2] {'dp'}, dimensions={0}, use_global_device_ids=true | all-gather | bytes 122880 | tf_op jit(solution)/shard_map/all_gather | solution.py:25
  158.6 0.1 fusion.35
  158.7 20.3 %all-gather.5 = f32[8,3,2048]{2,1,0:T(4,128)S(1)} all-gather(f32[1,3,2048]{2,1,0:T(4,128)S(1)} %maximum_bitcast_fusion.1), channel_id=3, replica_groups=mesh['dp'=4,'cls_0'=8,'cls_1'=4,'cls_2'=2] {'cls_0'}, dimensions={0}, use_global_device_ids=true | all-gather | bytes 221184 | tf_op jit(solution)/shard_map/all_gather | solution.py:25
  179.0 0.1 fusion.11
  179.1 0.2 fusion.13
  179.3 9.7 %all-gather.6 = f32[4,3,2048]{2,1,0:T(4,128)S(1)} all-gather(f32[1,3,2048]{2,1,0:T(4,128)S(1)} %maximum_bitcast_fusion.2), channel_id=4, replica_groups=mesh['dp'=4,'cls_0'=8,'cls_1'=4,'cls_2'=2] {'cls_1'}, dimensions={0}, use_global_device_ids=true | all-gather | bytes 122880 | tf_op jit(solution)/shard_map/all_gather | solution.py:25
  189.1 0.1 fusion.3
  189.2 13.8 %all-gather.7 = f32[2,3,2048]{2,1,0:T(4,128)S(1)} all-gather(f32[1,3,2048]{2,1,0:T(4,128)S(1)} %maximum_bitcast_fusion.3), channel_id=5, replica_groups=mesh['dp'=4,'cls_0'=8,'cls_1'=4,'cls_2'=2] {'cls_2'}, dimensions={0}, use_global_device_ids=true | all-gather | bytes 73728 | tf_op jit(solution)/shard_map/all_gather | solution.py:25
  203.1 0.6 dynamic-slice_subtract_fusion
  (15 shorter events, 0.3 us)
Async XLA Ops:
  6.5 58.3 %all-gather.10.cloned.1.call-start = ((), (), s32[]{:S(2)}) async-start(), calls=%async_computation | async-start | bytes 5242880 | tf_op jit(solution)/shard_map/all_gather | solution.py:87
  10.3 5.8 %copy-start.1 = (f32[4096,512]{1,0:T(8,128)S(1)}, f32[4096,512]{1,0:T(8,128)}, u32[]{:S(2)}) copy-start(f32[4096,512]{1,0:T(8,128)} %param.5) | copy-start | bytes 25165828
  19.6 13.0 %copy-start.3 = (s32[2048]{0:T(1024)S(1)}, s32[2048]{0:T(1024)}, u32[]{:S(2)}) copy-start(s32[2048]{0:T(1024)} %param.6) | copy-start | bytes 24580
  32.6 40.5 %copy-start.4 = (f32[2048]{0:T(1024)S(1)}, f32[2048]{0:T(1024)}, u32[]{:S(2)}) copy-start(f32[2048]{0:T(1024)} %param.7) | copy-start | bytes 24580
  64.8 4.7 %copy-start = (f32[2048,512]{1,0:T(8,128)S(1)}, f32[2048,512]{1,0:T(8,128)}, u32[]{:S(2)}) copy-start(f32[2048,512]{1,0:T(8,128)} %gather_fusion) | copy-start | bytes 12582916
  64.8 8.3 %slice-start = ((s8[8388608]{0:T(1024)(128)(4,1)}), s8[4194304]{0:T(1024)(128)(4,1)S(1)}, s32[]{:S(2)}) async-start(s8[8388608]{0:T(1024)(128)(4,1)} %bitcast.324), calls=%async_computation.1 | async-start | bytes 8388608
  64.8 8.4 %copy-start.2 = (f32[2048,512]{1,0:T(8,128)S(1)}, f32[2048,512]{1,0:T(8,128)}, u32[]{:S(2)}) copy-start(f32[2048,512]{1,0:T(8,128)} %all-gather.10.cloned.1.call-done) | copy-start | bytes 12582916
  69.5 5.2 %slice-start.1 = ((s8[8388608]{0:T(1024)(128)(4,1)}), s8[4194304]{0:T(1024)(128)(4,1)S(1)}, s32[]{:S(2)}) async-start(s8[8388608]{0:T(1024)(128)(4,1)} %bitcast.324), calls=%async_computation.2 | async-start | bytes 8388608
Sparse Core Ops, SparseCore 0:
  10.4 54.3 all-gather.9
where the time goes:
time: 211 us
  matrix products  59.6 us (28%)
  blocking collectives  52.9 us (25%)
  other arithmetic  36.4 us (17%)
  waiting for transfers between devices  32.2 us (15%)
  local copies, waits for them, and re-layouts  15.8 us (7%)
  between operations  13.6 us (6%)
    dot_general x1, matrix products, block_stats(): lax.dot_general(units, rows, (((1,), (1,)), ((), ())), precision=lax.Prec...  59.6 us
    all_gather x4, blocking collectives, gathered_once(): both, at, found = (lax.all_gather(jnp.concatenate(lines), axis), 0, {})  52.9 us
    all_gather x1, waiting for transfers between devices, body(): lax.all_gather(units_mine, 'dp', axis=0, tiled=True)  32.2 us
    reduce_sum x1, other arithmetic, block_stats(): total = jnp.sum(jnp.exp(logits - peak[:, None]), axis=1)  15.2 us
    gather x1, local copies, waits for them, and re-layouts, body(): picked = jnp.take(normed, local_all, axis=0)  12.9 us
    mul x2, other arithmetic, unit_rows(): values * lax.rsqrt(jnp.sum(values * values, axis=-1, keepdims=True) + 1e-06)  5.9 us
    reduce_sum x2, other arithmetic, unit_rows(): jnp.sum(values * values, axis=-1, keepdims=True) + 1e-06  5.52 us
  transfers between devices with their start and end apart: 1, of which 1 were waited for; matrix products, arithmetic and copies ran while one was open for 10% of the time, Pallas kernels for 0%

commit v1 on v0

v1 whole, which is shorter than its diff:
```python
import functools
import math

import jax
import jax.numpy as jnp
from jax import lax
from jax.experimental import pallas as pl
from jax.experimental.pallas import tpu as pltpu
from jax.sharding import Mesh
from jax.sharding import PartitionSpec as P

DP_CLS = ("dp", "cls_0", "cls_1", "cls_2")


MARGIN = 0.5
COS_MARGIN = math.cos(MARGIN)
SIN_MARGIN = math.sin(MARGIN)
EPS = 1e-06
LOG2E = math.log2(math.e)
LN2 = math.log(2.0)
LOWEST = -3e38

HALF = 256
TILE = 1024
SUB = 128
SLOTS = 32


def split(values):
    high = values.astype(jnp.bfloat16)
    return high, (values - high.astype(jnp.float32)).astype(jnp.bfloat16)


def owned_kernel(meta_ref, labels_ref, list_ref, *, rows_here):
    local = labels_ref[...] - meta_ref[2]
    lines, lanes = local.shape
    count = lines * lanes
    number = lax.broadcasted_iota(jnp.int32, local.shape, 0) * lanes
    number = number + lax.broadcasted_iota(jnp.int32, local.shape, 1)
    number = jnp.where((local >= 0) & (local < rows_here), number, count)

    def more(state):
        return state[1] < count

    def step(state):
        found, at = state
        list_ref[found] = at
        return found + 1, jnp.min(jnp.where(number > at, number, count))

    found, _ = lax.while_loop(more, step, (jnp.int32(0), jnp.min(number)))
    list_ref[count] = found


def owned(meta, labels, rows_here):
    count = labels.shape[0]
    return pl.pallas_call(
        functools.partial(owned_kernel, rows_here=rows_here),
        in_specs=[pl.BlockSpec(memory_space=pltpu.SMEM), pl.BlockSpec(memory_space=pltpu.VMEM)],
        out_specs=pl.BlockSpec(memory_space=pltpu.SMEM),
        out_shape=jax.ShapeDtypeStruct((count + 128,), jnp.int32),
        name="owned",
    )(meta, labels.reshape(-1, 128))


def half_ids(meta_ref, shift, ways):
    block = lax.rem(meta_ref[0] + (ways - shift), ways)
    swap = jnp.int32(0) if shift == 0 else meta_ref[1]
    return 2 * block + swap, 2 * block + 1 - swap


def start_target(k, number, meta_ref, labels_ref, rows_ref, sources, ways, found_ref, picked_ref, sems):
    place, core, offset = meta_ref[0], meta_ref[1], meta_ref[2]
    local = labels_ref[number] - offset
    at = pl.multiple_of((local // 8) * 8, 8)
    pltpu.make_async_copy(rows_ref.at[pl.ds(at, 8), :], picked_ref.at[k], sems.at[1, k]).start()
    half = number // HALF
    shift = lax.rem(place + ways - half // 2, ways)
    swapped = jnp.where(lax.rem(half, 2) == core, 0, 1)
    for (s, w), ref in sources.items():
        here = shift == s
        if w is not None:
            here = here & (swapped == w)

        @pl.when(here)
        def _(ref=ref):
            from_row = pl.multiple_of((lax.rem(number, ref.shape[0]) // 8) * 8, 8)
            pltpu.make_async_copy(ref.at[pl.ds(from_row, 8), :], found_ref.at[k], sems.at[0, k]).start()


def stats_kernel(meta_ref, *refs, shifts, ways, first, last):
    refs = list(refs)
    take = lambda n: [refs.pop(0) for _ in range(n)]
    labels_ref, scales_ref = take(2)
    halves = take(len(shifts) if first else 2 * len(shifts))
    if first:
        (rows_ref,) = take(1)
    else:
        high_ref, low_ref, before_ref = take(3)
    if last:
        list_ref, flat_labels_ref, flat_scales_ref, all_rows_ref = take(4)
        sources = {(0, None): refs.pop(0)}
        for s in range(1, ways):
            for w in range(2):
                sources[(s, w)] = refs.pop(0)
    (out_ref,) = take(1)
    if first:
        high_ref, low_ref = take(2)
    raw_ref, uh_ref, ul_ref, peak_ref, total_ref, local_ref, raw_sems = take(7)
    if last:
        found_ref, picked_ref, sems = take(3)
    step = pl.program_id(0)
    offset = meta_ref[2]
    ids = [i for s in shifts for i in half_ids(meta_ref, s, ways)]

    if last:
        limit = flat_labels_ref.shape[0]

        def begin(base, here):
            def one(k, carry):
                number = list_ref[base + k]
                start_target(
                    k, number, meta_ref, flat_labels_ref, all_rows_ref, sources, ways, found_ref, picked_ref, sems
                )
                return carry

            lax.fori_loop(0, here, one, 0)

        def finish(base, here):
            def wait(k, carry):
                rows = all_rows_ref.at[pl.ds(0, 8), :]
                pltpu.make_async_copy(rows, found_ref.at[k], sems.at[0, k]).wait()
                pltpu.make_async_copy(rows, picked_ref.at[k], sems.at[1, k]).wait()
                return carry

            lax.fori_loop(0, here, wait, 0)

            def one(k, carry):
                number = list_ref[base + k]
                local = flat_labels_ref[number] - offset
                values = found_ref[k, pl.ds(lax.rem(number, 8), 1), :]
                row = picked_ref[k, pl.ds(lax.rem(local, 8), 1), :]
                units = values * lax.rsqrt(jnp.sum(values * values, axis=1, keepdims=True) + EPS)
                row = row * lax.rsqrt(jnp.sum(row * row, axis=1, keepdims=True) + EPS)
                cosine = jnp.sum(units * row, axis=1, keepdims=True)
                across = units - cosine * row
                sine = jnp.sqrt(jnp.sum(across * across, axis=1, keepdims=True))
                target = flat_scales_ref[number] * (cosine * COS_MARGIN - sine * SIN_MARGIN)
                line = out_ref[number // HALF, pl.ds(1, 1), :]
                lane = lax.broadcasted_iota(jnp.int32, line.shape, 1)
                out_ref[number // HALF, pl.ds(1, 1), :] = jnp.where(lane == lax.rem(number, HALF), target, line)
                return carry

            lax.fori_loop(0, here, one, 0)

    @pl.when(step == 0)
    def _():
        if first:
            loads = [pltpu.make_async_copy(halves[0], raw_ref, raw_sems.at[0])]
        else:
            loads = [
                pltpu.make_async_copy(ref, raw_ref.at[pl.ds(h * HALF, HALF), :], raw_sems.at[h])
                for h, ref in enumerate(halves)
            ]
        for load in loads:
            load.start()
        if last:
            begin(0, jnp.minimum(list_ref[limit], SLOTS))
        for h in range(2 * len(shifts)):
            if h < len(loads):
                loads[h].wait()
            at = slice(h * HALF, (h + 1) * HALF)
            values = raw_ref[at, :].T
            inverse = lax.rsqrt(jnp.sum(values * values, axis=0, keepdims=True) + EPS)
            high, low = split(values * inverse * (scales_ref[ids[h]] * LOG2E))
            uh_ref[:, at] = high
            ul_ref[:, at] = low
            local_ref[:, at] = labels_ref[ids[h]] - offset
        peak_ref[...] = jnp.full_like(peak_ref, LOWEST)
        total_ref[...] = jnp.zeros_like(total_ref)

    peak, total = peak_ref[...], total_ref[...]
    width = peak.shape[1]
    uh, ul = uh_ref[...], ul_ref[...]
    local = jnp.broadcast_to(local_ref[...] - step * TILE, (8, width))
    local = local - lax.broadcasted_iota(jnp.int32, (8, width), 0)
    for k in range(TILE // SUB):
        at = slice(k * SUB, (k + 1) * SUB)
        if first:
            rows = rows_ref[at, :]
            rows = rows * lax.rsqrt(jnp.sum(rows * rows, axis=1, keepdims=True) + EPS)
            high, low = split(rows)
            high_ref[at, :] = high
            low_ref[at, :] = low
        else:
            high, low = high_ref[at, :], low_ref[at, :]
        logits = jnp.dot(high, uh, preferred_element_type=jnp.float32)
        logits = logits + jnp.dot(low, uh, preferred_element_type=jnp.float32)
        logits = logits + jnp.dot(high, ul, preferred_element_type=jnp.float32)
        parts = [
            jnp.where(local == k * SUB + 8 * g, LOWEST, logits[8 * g : 8 * g + 8]) for g in range(SUB // 8)
        ]
        tops = list(parts)
        while len(tops) > 1:
            tops = [jnp.maximum(a, b) for a, b in zip(tops[::2], tops[1::2])]
        above = jnp.maximum(peak, tops[0])
        sums = [jnp.exp2(part - above) for part in parts]
        while len(sums) > 1:
            sums = [a + b for a, b in zip(sums[::2], sums[1::2])]
        total = total * jnp.exp2(peak - above) + sums[0]
        peak = above
    peak_ref[...] = peak
    total_ref[...] = total

    @pl.when(step == pl.num_programs(0) - 1)
    def _():
        top = jnp.max(peak, axis=0, keepdims=True)
        full = jnp.sum(total * jnp.exp2(peak - top), axis=0, keepdims=True)
        level = top + jnp.log2(full)
        if first:
            out_ref[...] = jnp.zeros_like(out_ref)
        else:
            out_ref[...] = before_ref[...]
        for h, i in enumerate(ids):
            out_ref[i, pl.ds(0, 1), :] = level[:, h * HALF : (h + 1) * HALF]
        if last:
            found = list_ref[limit]
            finish(0, jnp.minimum(found, SLOTS))

            def batch(b, carry):
                here = jnp.minimum(found - b * SLOTS, SLOTS)
                begin(b * SLOTS, here)
                finish(b * SLOTS, here)
                return carry

            lax.fori_loop(1, (found + SLOTS - 1) // SLOTS, batch, 0)


def stats(meta, labels, scales, shifts, halves, rows, ways, before=None, extra=None):
    first, last = before is None, extra is not None
    rows_here, width = rows[0].shape
    blocks = labels.shape[0]
    lines = 2 * HALF * len(shifts)
    whole = lambda *shape: pl.BlockSpec(shape, lambda t, meta: (0,) * len(shape))
    far = pl.BlockSpec(memory_space=pl.ANY)
    scalars = pl.BlockSpec(memory_space=pltpu.SMEM)
    tiles = pl.BlockSpec((TILE, width), lambda t, meta: (t, 0))
    in_specs = [whole(blocks, 1, HALF), whole(blocks, 1, HALF)] + [far] * len(halves) + [tiles] * len(rows)
    args = [labels, scales, *halves, *rows]
    out_specs = [whole(blocks, 2, HALF)]
    out_shape = [jax.ShapeDtypeStruct((blocks, 2, HALF), jnp.float32)]
    scratch = [
        pltpu.VMEM((lines, width), jnp.float32),
        pltpu.VMEM((width, lines), jnp.bfloat16),
        pltpu.VMEM((width, lines), jnp.bfloat16),
        pltpu.VMEM((8, lines), jnp.float32),
        pltpu.VMEM((8, lines), jnp.float32),
        pltpu.VMEM((1, lines), jnp.int32),
        pltpu.SemaphoreType.DMA((2 * len(shifts),)),
    ]
    if first:
        out_specs += [tiles, tiles]
        out_shape += [jax.ShapeDtypeStruct((rows_here, width), jnp.bfloat16)] * 2
    else:
        in_specs.append(whole(blocks, 2, HALF))
        args.append(before)
    if last:
        in_specs += [scalars] * 3 + [far] * (len(extra) - 3)
        args += extra
        scratch += [
            pltpu.VMEM((SLOTS, 8, width), jnp.float32),
            pltpu.VMEM((SLOTS, 8, width), jnp.float32),
            pltpu.SemaphoreType.DMA((2, SLOTS)),
        ]
    return pl.pallas_call(
        functools.partial(stats_kernel, shifts=shifts, ways=ways, first=first, last=last),
        grid_spec=pltpu.PrefetchScalarGridSpec(
            num_scalar_prefetch=1,
            grid=(rows_here // TILE,),
            in_specs=in_specs,
            out_specs=out_specs,
            scratch_shapes=scratch,
        ),
        out_shape=out_shape,
        compiler_params=pltpu.CompilerParams(dimension_semantics=("arbitrary",)),
    )(meta, *args)


def body(embeddings, classifier, labels, row_scale):
    rows_here = classifier.shape[0]
    count = labels.shape[0]
    ways = lax.axis_size("dp")
    core = lax.axis_index("cls_2")
    meta = jnp.stack([lax.axis_index("dp"), core, lax.axis_index(DP_CLS) * rows_here]).astype(jnp.int32)
    swap = lambda part: lax.ppermute(part, "cls_2", [(0, 1), (1, 0)])
    shift = lambda part, k: lax.ppermute(part, "dp", [(i, (i + k) % ways) for i in range(ways)])

    label_blocks = labels.reshape(-1, 1, HALF)
    scale_blocks = row_scale.reshape(-1, 1, HALF)
    mine = lax.dynamic_slice_in_dim(embeddings, core * HALF, HALF, 0)
    left = shift(mine, 1)
    right = shift(mine, 3)
    across = shift(mine, 2)
    numbers = owned(meta, labels, rows_here)
    held, high, low = stats(meta, label_blocks, scale_blocks, (0,), (embeddings,), (classifier,), ways)
    near = (left, swap(left), right, swap(right))
    (held,) = stats(meta, label_blocks, scale_blocks, (1, 3), near, (high, low), ways, held)
    far = (across, swap(across))
    extra = [numbers, labels, row_scale, classifier, embeddings, near[0], near[1], *far, near[2], near[3]]
    (held,) = stats(meta, label_blocks, scale_blocks, (2,), far, (high, low), ways, held, extra)

    devices = lax.axis_size(DP_CLS)
    share = count // devices
    send = held.reshape(-1, 2, HALF // share, share).transpose(0, 2, 1, 3).reshape(devices, 2 * share)
    got = lax.all_to_all(send, DP_CLS, 0, 0, tiled=True)
    level, target = got[:, :share], jnp.sum(got[:, share:], axis=0)
    top = jnp.max(level, axis=0)
    peak = jnp.maximum(top * LN2, target)
    total = jnp.sum(jnp.exp2(level - top), axis=0) * jnp.exp(top * LN2 - peak) + jnp.exp(target - peak)
    return peak + jnp.log(total) - target


def solution(mesh):
    torus = Mesh(mesh.devices.reshape(mesh.shape["dp"], 8, 4, 2), ("dp", "cls_0", "cls_1", "cls_2"))
    return jax.shard_map(
        body,
        mesh=torus,
        in_specs=(P("dp", None), P(DP_CLS, None), P(), P()),
        out_specs=P(DP_CLS),
        check_vma=False,
    )
```

time: 211 us -> 117 us (0.55)
  matrix products: 59.6 us -> 0 us
  Pallas kernels: 0 us -> 54.3 us
  other arithmetic: 36.4 us -> 1.52 us
  blocking collectives: 52.9 us -> 26.3 us
  waiting for transfers between devices: 32.2 us -> 11.8 us
  starting transfers between devices: 0.01 us -> 18.4 us
  between operations: 13.6 us -> 0.14 us
  local copies, waits for them, and re-layouts: 15.8 us -> 4.1 us
    dot_general x1 -> x0, matrix products: 59.6 us -> none  [block_stats(): lax.dot_general(units, rows, (((1,), (1,)), ((), ())), precision=lax.Prec...]
    pallas_call x0 -> x4, Pallas kernels: none -> 54.3 us  [the longest x3 50.3 us: stats(): pl.pallas_call(functools.partial(stats_kernel, shifts=shifts, ways=ways,...]
    all_gather x4 -> x0, blocking collectives: 52.9 us -> none  [gathered_once(): both, at, found = (lax.all_gather(jnp.concatenate(lines), axis), 0, {})]
    all_gather x1 -> x0, waiting for transfers between devices: 32.2 us -> none  [body(): lax.all_gather(units_mine, 'dp', axis=0, tiled=True)]
    reduce_sum x5 -> x1, other arithmetic: 28.4 us -> 0.19 us  [body(): jnp.sum(jnp.exp2(level - top), axis=0) * jnp.exp(top * LN2 - peak)]
    all_to_all x0 -> x1, blocking collectives: none -> 26.3 us  [body(): got = lax.all_to_all(send, DP_CLS, 0, 0, tiled=True)]
    ppermute x0 -> x6, starting transfers between devices: none -> 18.4 us  [the longest x3 13.3 us: body(): swap = lambda part: lax.ppermute(part, 'cls_2', [(0, 1), (1, 0)])]
    gather x1 -> x0, local copies, waits for them, and re-layouts: 12.9 us -> none  [body(): picked = jnp.take(normed, local_all, axis=0)]
  transfers between devices with their start and end apart: 1 -> 6, of which waited for: 1 -> 1; matrix products, arithmetic and copies ran while one was open for 10% -> 1% of each run, Pallas kernels for 0% -> 32%
where the time goes in v1:
time: 117 us
  Pallas kernels  54.3 us (46%)
  blocking collectives  26.3 us (22%)
  starting transfers between devices  18.4 us (16%)
  waiting for transfers between devices  11.8 us (10%)
  local copies, waits for them, and re-layouts  4.1 us (4%)
  other arithmetic  1.52 us (1%)
    pallas_call x3, Pallas kernels, stats(): pl.pallas_call(functools.partial(stats_kernel, shifts=shifts, ways=ways,...  50.3 us
    all_to_all x1, blocking collectives, body(): got = lax.all_to_all(send, DP_CLS, 0, 0, tiled=True)  26.3 us
    ppermute x3, starting transfers between devices, body(): swap = lambda part: lax.ppermute(part, 'cls_2', [(0, 1), (1, 0)])  13.3 us
    ppermute x3, waiting for transfers between devices, body(): lax.ppermute(part, 'dp', [(i, (i + k) % ways) for i in range(ways)])  11.8 us
    ppermute x3, starting transfers between devices, body(): lax.ppermute(part, 'dp', [(i, (i + k) % ways) for i in range(ways)])  5.1 us
    pallas_call x1, Pallas kernels, owned(): pl.pallas_call(functools.partial(owned_kernel, rows_here=rows_here), in_s...  3.96 us
  transfers between devices with their start and end apart: 6, of which 1 were waited for; matrix products, arithmetic and copies ran while one was open for 1% of the time, Pallas kernels for 32%

profile of v1, /device:TPU:1, one launch (start us, length us, event | category | flops | bytes accessed | tf_op | source)
XLA Modules:
  0.0 116.6 jit_solution(6841242683855223695)
XLA Ops:
  0.0 1.1 constant_dynamic-slice_fusion
  1.1 3.4 %collective-permute-start.4 = (f32[256,512]{1,0:T(8,128)S(1)}, f32[256,512]{1,0:T(8,128)S(1)}, u32[]{:S(2)}, u32[]{:S(2)}) collective-permute-start(f32[256,512]{1,0:T(8,128)S(1)} %constant_dynamic-slice_fusion), channel_id=1, source_target_pairs={{0,192},{64,0},{128,64},{192,128},{1,193},{65,1},{129,65},{193,129... | collective-permute-start | bytes 1572872 | tf_op jit(solution)/shard_map/ppermute | solution.py:295
  4.5 0.0 collective-permute-start.2
  4.5 1.7 %collective-permute-start = (f32[256,512]{1,0:T(8,128)S(1)}, f32[256,512]{1,0:T(8,128)S(1)}, u32[]{:S(2)}, u32[]{:S(2)}) collective-permute-start(f32[256,512]{1,0:T(8,128)S(1)} %constant_dynamic-slice_fusion), channel_id=1, source_target_pairs={{0,128},{64,192},{128,0},{192,64},{1,129},{65,193},{129,1},{193,65... | collective-permute-start | bytes 1572872 | tf_op jit(solution)/shard_map/ppermute | solution.py:295
  6.2 11.8 %collective-permute-done.4.refs_4_.refs_16_ = f32[256,512]{1,0:T(8,128)S(1)} collective-permute-done((f32[256,512]{1,0:T(8,128)S(1)}, f32[256,512]{1,0:T(8,128)S(1)}, u32[]{:S(2)}, u32[]{:S(2)}) %collective-permute-start.4) | collective-permute-done | bytes 524320 | tf_op jit(solution)/shard_map/ppermute | solution.py:295
  18.0 0.0 copy-start.2
  18.0 9.8 %collective-permute-start.5 = (f32[256,512]{1,0:T(8,128)S(1)}, f32[256,512]{1,0:T(8,128)S(1)}, u32[]{:S(2)}, u32[]{:S(2)}) collective-permute-start(f32[256,512]{1,0:T(8,128)S(1)} %collective-permute-done.4.refs_4_.refs_16_), channel_id=1, source_target_pairs={{0,1},{1,0},{2,3},{3,2},{4,5},{5,4},{6,7},{7,6},{8,9},{9,8},{10,11... | collective-permute-start | bytes 1572872 | tf_op jit(solution)/shard_map/ppermute | solution.py:294
  27.8 0.0 collective-permute-done.2.refs_2_.refs_12_
  27.8 0.0 copy-start.3
  27.8 3.4 %collective-permute-start.3 = (f32[256,512]{1,0:T(8,128)S(1)}, f32[256,512]{1,0:T(8,128)S(1)}, u32[]{:S(2)}, u32[]{:S(2)}) collective-permute-start(f32[256,512]{1,0:T(8,128)S(1)} %collective-permute-done.2.refs_2_.refs_12_), channel_id=1, source_target_pairs={{0,1},{1,0},{2,3},{3,2},{4,5},{5,4},{6,7},{7,6},{8,9},{9,8},{10,11... | collective-permute-start | bytes 1572872 | tf_op jit(solution)/shard_map/ppermute | solution.py:294
  31.2 0.0 collective-permute-done.refs_2_.refs_14_
  31.2 0.0 copy-start
  31.2 0.1 collective-permute-start.1
  31.3 0.7 pad_add_fusion.meta_ref
  32.0 4.0 %owned.1.refs_7_ = s32[2176]{0:T(1024)} custom-call(s32[3]{0:T(128)} %pad_add_fusion.meta_ref, s32[16,128]{1,0:T(8,128)} %bitcast.15), custom_call_target="tpu_custom_call" | custom-call | tf_op jit(solution)/shard_map/owned/pallas_call | solution.py:56
  36.0 14.0 %shard_map.46 = (f32[8,2,256]{2,1,0:T(2,128)}, bf16[4096,512]{1,0:T(8,128)(2,1)}, bf16[4096,512]{1,0:T(8,128)(2,1)}) custom-call(s32[3]{0:T(128)} %pad_add_fusion.meta_ref, s32[8,1,256]{2,1,0:T(1,128)} %bitcast.16, f32[8,1,256]{2,1,0:T(1,128)} %bitcast.19, f32[512,512]{1,0:T(8,128)} %refs_11_.1, f32[4096,512]{1,0:T(8,128)} %refs_10_.1), custom_call_target="tpu_custom_call" | custom-call | tf_op jit(solution)/shard_map/pallas_call | solution.py:274
  50.0 0.0 copy-done.2
  50.0 0.0 copy-done.3
  50.0 0.0 copy-done
  50.0 0.0 collective-permute-done.5.refs_5_.refs_17_
  50.0 0.0 copy-start.4
  50.0 0.0 collective-permute-done.3.refs_3_.refs_13_
  50.0 0.0 copy-start.5
  50.1 0.8 copy-done.4
  50.8 0.2 copy-done.5
  51.0 19.9 %shard_map.47.refs_6_ = f32[8,2,256]{2,1,0:T(2,128)} custom-call(s32[3]{0:T(128)} %pad_add_fusion.meta_ref, s32[8,1,256]{2,1,0:T(1,128)} %bitcast.17, f32[8,1,256]{2,1,0:T(1,128)} %bitcast.20, f32[256,512]{1,0:T(8,128)} %copy-done.3, f32[256,512]{1,0:T(8,128)} %copy-done.5, f32[256,512]{1,0:T(8,128)} %copy-done.2, f32[256,512]{1,0:T(8,128)} %copy-done.4, ...), custom_call_target="tpu_custom_call" | custom-call | tf_op jit(solution)/shard_map/pallas_call | solution.py:274
  70.9 0.0 collective-permute-done.1.refs_3_.refs_15_
  70.9 0.0 copy-start.1
  70.9 0.8 copy-done.1
  71.7 16.4 %shard_map.48 = f32[8,2,256]{2,1,0:T(2,128)} custom-call(s32[3]{0:T(128)} %pad_add_fusion.meta_ref, s32[8,1,256]{2,1,0:T(1,128)} %bitcast.18, f32[8,1,256]{2,1,0:T(1,128)} %bitcast.21, f32[256,512]{1,0:T(8,128)} %copy-done, f32[256,512]{1,0:T(8,128)} %copy-done.1, bf16[4096,512]{1,0:T(8,128)(2,1)} %get-tuple-element.8.refs_6_.refs_4_, ...), custom_call_target="tpu_custom_call" | custom-call | tf_op jit(solution)/shard_map/pallas_call | solution.py:274
  88.2 0.7 copy.10
  88.9 0.2 reshape.20
  89.1 0.1 copy.11
  89.2 0.1 all_to_all.8
  89.3 0.1 copy.12
  89.4 26.3 %all_to_all.12 = f32[256,1,16]{2,1,0:T(1,128)S(1)} all-to-all(f32[256,1,16]{2,1,0:T(1,128)S(1)} %copy.12), channel_id=1, replica_groups=mesh['dp'=4,'cls_0'=8,'cls_1'=4,'cls_2'=2] {'dp','cls_0','cls_1','cls_2'}, dimensions={0} | all-to-all | bytes 32768 | tf_op jit(solution)/shard_map/all_to_all | solution.py:314
  115.7 0.1 copy.13
  115.8 0.1 slice_reduce_fusion.1
  115.9 0.2 exponential_reduce_fusion
  116.1 0.5 add_subtract_fusion
Async XLA Ops:
  1.1 16.9 %collective-permute-start.4 = (f32[256,512]{1,0:T(8,128)S(1)}, f32[256,512]{1,0:T(8,128)S(1)}, u32[]{:S(2)}, u32[]{:S(2)}) collective-permute-start(f32[256,512]{1,0:T(8,128)S(1)} %constant_dynamic-slice_fusion), channel_id=1, source_target_pairs={{0,192},{64,0},{128,64},{192,128},{1,193},{65,1},{129,65},{193,129... | collective-permute-start | bytes 1572872 | tf_op jit(solution)/shard_map/ppermute | solution.py:295
  4.5 23.4 %collective-permute-start.2 = (f32[256,512]{1,0:T(8,128)S(1)}, f32[256,512]{1,0:T(8,128)S(1)}, u32[]{:S(2)}, u32[]{:S(2)}) collective-permute-start(f32[256,512]{1,0:T(8,128)S(1)} %constant_dynamic-slice_fusion), channel_id=1, source_target_pairs={{0,64},{64,128},{128,192},{192,0},{1,65},{65,129},{129,193},{193,1... | collective-permute-start | bytes 1572872 | tf_op jit(solution)/shard_map/ppermute | solution.py:295
  4.5 26.8 %collective-permute-start = (f32[256,512]{1,0:T(8,128)S(1)}, f32[256,512]{1,0:T(8,128)S(1)}, u32[]{:S(2)}, u32[]{:S(2)}) collective-permute-start(f32[256,512]{1,0:T(8,128)S(1)} %constant_dynamic-slice_fusion), channel_id=1, source_target_pairs={{0,128},{64,192},{128,0},{192,64},{1,129},{65,193},{129,1},{193,65... | collective-permute-start | bytes 1572872 | tf_op jit(solution)/shard_map/ppermute | solution.py:295
  18.0 32.0 %copy-start.2 = (f32[256,512]{1,0:T(8,128)}, f32[256,512]{1,0:T(8,128)S(1)}, u32[]{:S(2)}) copy-start(f32[256,512]{1,0:T(8,128)S(1)} %collective-permute-done.4.refs_4_.refs_16_) | copy-start | bytes 1572868
  18.0 32.0 %collective-permute-start.5 = (f32[256,512]{1,0:T(8,128)S(1)}, f32[256,512]{1,0:T(8,128)S(1)}, u32[]{:S(2)}, u32[]{:S(2)}) collective-permute-start(f32[256,512]{1,0:T(8,128)S(1)} %collective-permute-done.4.refs_4_.refs_16_), channel_id=1, source_target_pairs={{0,1},{1,0},{2,3},{3,2},{4,5},{5,4},{6,7},{7,6},{8,9},{9,8},{10,11... | collective-permute-start | bytes 1572872 | tf_op jit(solution)/shard_map/ppermute | solution.py:294
  27.8 22.2 %copy-start.3 = (f32[256,512]{1,0:T(8,128)}, f32[256,512]{1,0:T(8,128)S(1)}, u32[]{:S(2)}) copy-start(f32[256,512]{1,0:T(8,128)S(1)} %collective-permute-done.2.refs_2_.refs_12_) | copy-start | bytes 1572868
  27.8 22.2 %collective-permute-start.3 = (f32[256,512]{1,0:T(8,128)S(1)}, f32[256,512]{1,0:T(8,128)S(1)}, u32[]{:S(2)}, u32[]{:S(2)}) collective-permute-start(f32[256,512]{1,0:T(8,128)S(1)} %collective-permute-done.2.refs_2_.refs_12_), channel_id=1, source_target_pairs={{0,1},{1,0},{2,3},{3,2},{4,5},{5,4},{6,7},{7,6},{8,9},{9,8},{10,11... | collective-permute-start | bytes 1572872 | tf_op jit(solution)/shard_map/ppermute | solution.py:294
  31.2 18.8 %copy-start = (f32[256,512]{1,0:T(8,128)}, f32[256,512]{1,0:T(8,128)S(1)}, u32[]{:S(2)}) copy-start(f32[256,512]{1,0:T(8,128)S(1)} %collective-permute-done.refs_2_.refs_14_) | copy-start | bytes 1572868
  31.2 39.7 %collective-permute-start.1 = (f32[256,512]{1,0:T(8,128)S(1)}, f32[256,512]{1,0:T(8,128)S(1)}, u32[]{:S(2)}, u32[]{:S(2)}) collective-permute-start(f32[256,512]{1,0:T(8,128)S(1)} %collective-permute-done.refs_2_.refs_14_), channel_id=1, source_target_pairs={{0,1},{1,0},{2,3},{3,2},{4,5},{5,4},{6,7},{7,6},{8,9},{9,8},{10,11... | collective-permute-start | bytes 1572872 | tf_op jit(solution)/shard_map/ppermute | solution.py:294
  50.0 0.8 copy-start.4
  50.0 1.0 copy-start.5
  70.9 0.8 copy-start.1

commit v2 on v1

--- a/solution.py
+++ b/solution.py
@@ -22,13 +22,18 @@
 
 HALF = 256
 TILE = 1024
-SUB = 128
+SUB = 256
 SLOTS = 32
+CHAINS = 4
 
 
 def split(values):
     high = values.astype(jnp.bfloat16)
     return high, (values - high.astype(jnp.float32)).astype(jnp.bfloat16)
+
+
+def product(a, b):
+    return lax.dot_general(a, b, (((1,), (1,)), ((), ())), preferred_element_type=jnp.float32)
 
 
 def owned_kernel(meta_ref, labels_ref, list_ref, *, rows_here):
@@ -39,15 +44,24 @@
     number = number + lax.broadcasted_iota(jnp.int32, local.shape, 1)
     number = jnp.where((local >= 0) & (local < rows_here), number, count)
 
+    chains = [number[q * lines // CHAINS : (q + 1) * lines // CHAINS] for q in range(CHAINS)]
+
+    def step(state):
+        found, heads = state
+        for head in heads:
+            here = head < count
+
+            @pl.when(here)
+            def _(found=found, head=head):
+                list_ref[found] = head
+
+            found = found + here.astype(jnp.int32)
+        return found, [jnp.min(jnp.where(part > head, part, count)) for part, head in zip(chains, heads)]
+
     def more(state):
-        return state[1] < count
-
-    def step(state):
-        found, at = state
-        list_ref[found] = at
-        return found + 1, jnp.min(jnp.where(number > at, number, count))
-
-    found, _ = lax.while_loop(more, step, (jnp.int32(0), jnp.min(number)))
+        return functools.reduce(jnp.minimum, state[1]) < count
+
+    found, _ = lax.while_loop(more, step, (jnp.int32(0), [jnp.min(part) for part in chains]))
     list_ref[count] = found
 
 
@@ -107,7 +121,7 @@
         high_ref, low_ref = take(2)
     raw_ref, uh_ref, ul_ref, peak_ref, total_ref, local_ref, raw_sems = take(7)
     if last:
-        found_ref, picked_ref, sems = take(3)
+        found_ref, picked_ref, group_ref, sems = take(4)
     step = pl.program_id(0)
     offset = meta_ref[2]
     ids = [i for s in shifts for i in half_ids(meta_ref, s, ways)]
@@ -134,23 +148,37 @@
 
             lax.fori_loop(0, here, wait, 0)
 
-            def one(k, carry):
-                number = list_ref[base + k]
-                local = flat_labels_ref[number] - offset
-                values = found_ref[k, pl.ds(lax.rem(number, 8), 1), :]
-                row = picked_ref[k, pl.ds(lax.rem(local, 8), 1), :]
-                units = values * lax.rsqrt(jnp.sum(values * values, axis=1, keepdims=True) + EPS)
-                row = row * lax.rsqrt(jnp.sum(row * row, axis=1, keepdims=True) + EPS)
-                cosine = jnp.sum(units * row, axis=1, keepdims=True)
-                across = units - cosine * row
+            def eight(g, carry):
+                first_slot = g * 8
+                numbers = []
+                for k in range(8):
+                    slot = first_slot + k
+                    number = jnp.where(slot < here, list_ref[base + slot], 0)
+                    local = jnp.maximum(flat_labels_ref[number] - offset, 0)
+                    group_ref[0, k : k + 1, :] = found_ref[slot, pl.ds(lax.rem(number, 8), 1), :]
+                    group_ref[1, k : k + 1, :] = picked_ref[slot, pl.ds(lax.rem(local, 8), 1), :]
+                    numbers.append(number)
+                units, picked = group_ref[0], group_ref[1]
+                units = units * lax.rsqrt(jnp.sum(units * units, axis=1, keepdims=True) + EPS)
+                picked = picked * lax.rsqrt(jnp.sum(picked * picked, axis=1, keepdims=True) + EPS)
+                cosine = jnp.sum(units * picked, axis=1, keepdims=True)
+                across = units - cosine * picked
                 sine = jnp.sqrt(jnp.sum(across * across, axis=1, keepdims=True))
-                target = flat_scales_ref[number] * (cosine * COS_MARGIN - sine * SIN_MARGIN)
-                line = out_ref[number // HALF, pl.ds(1, 1), :]
-                lane = lax.broadcasted_iota(jnp.int32, line.shape, 1)
-                out_ref[number // HALF, pl.ds(1, 1), :] = jnp.where(lane == lax.rem(number, HALF), target, line)
+                margin = cosine * COS_MARGIN - sine * SIN_MARGIN
+                for k in range(8):
+                    number = numbers[k]
+
+                    @pl.when(first_slot + k < here)
+                    def _(k=k, number=number):
+                        target = flat_scales_ref[number] * margin[k : k + 1]
+                        line = out_ref[number // HALF, pl.ds(1, 1), :]
+                        lane = lax.broadcasted_iota(jnp.int32, line.shape, 1)
+                        line = jnp.where(lane == lax.rem(number, HALF), target, line)
+                        out_ref[number // HALF, pl.ds(1, 1), :] = line
+
                 return carry
 
-            lax.fori_loop(0, here, one, 0)
+            lax.fori_loop(0, (here + 7) // 8, eight, 0)
 
     @pl.when(step == 0)
     def _():
@@ -169,11 +197,12 @@
             if h < len(loads):
                 loads[h].wait()
             at = slice(h * HALF, (h + 1) * HALF)
-            values = raw_ref[at, :].T
-            inverse = lax.rsqrt(jnp.sum(values * values, axis=0, keepdims=True) + EPS)
-            high, low = split(values * inverse * (scales_ref[ids[h]] * LOG2E))
-            uh_ref[:, at] = high
-            ul_ref[:, at] = low
+            values = raw_ref[at, :]
+            inverse = lax.rsqrt(jnp.sum(values * values, axis=1, keepdims=True) + EPS)
+            scale = jnp.broadcast_to(scales_ref[ids[h]] * LOG2E, (8, HALF)).T[:, :1]
+            high, low = split(values * (inverse * scale))
+            uh_ref[at, :] = high
+            ul_ref[at, :] = low
             local_ref[:, at] = labels_ref[ids[h]] - offset
         peak_ref[...] = jnp.full_like(peak_ref, LOWEST)
         total_ref[...] = jnp.zeros_like(total_ref)
@@ -193,9 +222,7 @@
             low_ref[at, :] = low
         else:
             high, low = high_ref[at, :], low_ref[at, :]
-        logits = jnp.dot(high, uh, preferred_element_type=jnp.float32)
-        logits = logits + jnp.dot(low, uh, preferred_element_type=jnp.float32)
-        logits = logits + jnp.dot(high, ul, preferred_element_type=jnp.float32)
+        logits = product(high, uh) + product(low, uh) + product(high, ul)
         parts = [
             jnp.where(local == k * SUB + 8 * g, LOWEST, logits[8 * g : 8 * g + 8]) for g in range(SUB // 8)
         ]
@@ -250,8 +277,8 @@
     out_shape = [jax.ShapeDtypeStruct((blocks, 2, HALF), jnp.float32)]
     scratch = [
         pltpu.VMEM((lines, width), jnp.float32),
-        pltpu.VMEM((width, lines), jnp.bfloat16),
-        pltpu.VMEM((width, lines), jnp.bfloat16),
+        pltpu.VMEM((lines, width), jnp.bfloat16),
+        pltpu.VMEM((lines, width), jnp.bfloat16),
         pltpu.VMEM((8, lines), jnp.float32),
         pltpu.VMEM((8, lines), jnp.float32),
         pltpu.VMEM((1, lines), jnp.int32),
@@ -269,6 +296,7 @@
         scratch += [
             pltpu.VMEM((SLOTS, 8, width), jnp.float32),
             pltpu.VMEM((SLOTS, 8, width), jnp.float32),
+            pltpu.VMEM((2, 8, width), jnp.float32),
             pltpu.SemaphoreType.DMA((2, SLOTS)),
         ]
     return pl.pallas_call(
@@ -302,7 +330,8 @@
     across = shift(mine, 2)
     numbers = owned(meta, labels, rows_here)
     held, high, low = stats(meta, label_blocks, scale_blocks, (0,), (embeddings,), (classifier,), ways)
-    near = (left, swap(left), right, swap(right))
+    left_other = swap(left)
+    near = (left, left_other, right, swap(right))
     (held,) = stats(meta, label_blocks, scale_blocks, (1, 3), near, (high, low), ways, held)
     far = (across, swap(across))
     extra = [numbers, labels, row_scale, classifier, embeddings, near[0], near[1], *far, near[2], near[3]]

time: 117 us -> 113 us (0.966)
  blocking collectives: 26.3 us -> 24 us
  Pallas kernels: 54.3 us -> 52.1 us
    all_to_all x1, blocking collectives: 26.3 us -> 24 us  [body(): got = lax.all_to_all(send, DP_CLS, 0, 0, tiled=True)]
    pallas_call x3, Pallas kernels: 50.3 us -> 48.7 us  [stats(): pl.pallas_call(functools.partial(stats_kernel, shifts=shifts, ways=ways,...]
  transfers between devices with their start and end apart: 6 -> 6, of which waited for: 1 -> 1; matrix products, arithmetic and copies ran while one was open for 1% -> 1% of each run, Pallas kernels for 32% -> 34%
where the time goes in v2:
time: 113 us; the launch traced here: 112 us
  Pallas kernels  52.1 us (46%)
  blocking collectives  24 us (21%)
  starting transfers between devices  18.4 us (16%)
  waiting for transfers between devices  11.8 us (10%)
  local copies, waits for them, and re-layouts  4.1 us (4%)
  other arithmetic  1.52 us (1%)
    pallas_call x3, Pallas kernels, stats(): pl.pallas_call(functools.partial(stats_kernel, shifts=shifts, ways=ways,...  48.7 us
    all_to_all x1, blocking collectives, body(): got = lax.all_to_all(send, DP_CLS, 0, 0, tiled=True)  24 us
    ppermute x3, starting transfers between devices, body(): swap = lambda part: lax.ppermute(part, 'cls_2', [(0, 1), (1, 0)])  13.3 us
    ppermute x3, waiting for transfers between devices, body(): lax.ppermute(part, 'dp', [(i, (i + k) % ways) for i in range(ways)])  11.8 us
    ppermute x3, starting transfers between devices, body(): lax.ppermute(part, 'dp', [(i, (i + k) % ways) for i in range(ways)])  5.1 us
    pallas_call x1, Pallas kernels, owned(): pl.pallas_call(functools.partial(owned_kernel, rows_here=rows_here), in_s...  3.42 us
  transfers between devices with their start and end apart: 6, of which 1 were waited for; matrix products, arithmetic and copies ran while one was open for 1% of the time, Pallas kernels for 34%

profile of v2, /device:TPU:1, one launch (start us, length us, event | category | flops | bytes accessed | tf_op | source)
XLA Modules:
  0.0 112.2 jit_solution(8543909237256855327)
XLA Ops:
  0.0 1.1 constant_dynamic-slice_fusion
  1.1 3.4 %collective-permute-start.4 = (f32[256,512]{1,0:T(8,128)S(1)}, f32[256,512]{1,0:T(8,128)S(1)}, u32[]{:S(2)}, u32[]{:S(2)}) collective-permute-start(f32[256,512]{1,0:T(8,128)S(1)} %constant_dynamic-slice_fusion), channel_id=1, source_target_pairs={{0,192},{64,0},{128,64},{192,128},{1,193},{65,1},{129,65},{193,129... | collective-permute-start | bytes 1572872 | tf_op jit(solution)/shard_map/ppermute | solution.py:323
  4.5 0.0 collective-permute-start.2
  4.5 1.7 %collective-permute-start = (f32[256,512]{1,0:T(8,128)S(1)}, f32[256,512]{1,0:T(8,128)S(1)}, u32[]{:S(2)}, u32[]{:S(2)}) collective-permute-start(f32[256,512]{1,0:T(8,128)S(1)} %constant_dynamic-slice_fusion), channel_id=1, source_target_pairs={{0,128},{64,192},{128,0},{192,64},{1,129},{65,193},{129,1},{193,65... | collective-permute-start | bytes 1572872 | tf_op jit(solution)/shard_map/ppermute | solution.py:323
  6.2 11.8 %collective-permute-done.4.refs_4_.refs_16_ = f32[256,512]{1,0:T(8,128)S(1)} collective-permute-done((f32[256,512]{1,0:T(8,128)S(1)}, f32[256,512]{1,0:T(8,128)S(1)}, u32[]{:S(2)}, u32[]{:S(2)}) %collective-permute-start.4) | collective-permute-done | bytes 524320 | tf_op jit(solution)/shard_map/ppermute | solution.py:323
  18.0 0.0 copy-start.2
  18.0 9.8 %collective-permute-start.5 = (f32[256,512]{1,0:T(8,128)S(1)}, f32[256,512]{1,0:T(8,128)S(1)}, u32[]{:S(2)}, u32[]{:S(2)}) collective-permute-start(f32[256,512]{1,0:T(8,128)S(1)} %collective-permute-done.4.refs_4_.refs_16_), channel_id=1, source_target_pairs={{0,1},{1,0},{2,3},{3,2},{4,5},{5,4},{6,7},{7,6},{8,9},{9,8},{10,11... | collective-permute-start | bytes 1572872 | tf_op jit(solution)/shard_map/ppermute | solution.py:322
  27.8 0.0 collective-permute-done.2.refs_2_.refs_12_
  27.8 0.0 copy-start.3
  27.8 3.4 %collective-permute-start.3 = (f32[256,512]{1,0:T(8,128)S(1)}, f32[256,512]{1,0:T(8,128)S(1)}, u32[]{:S(2)}, u32[]{:S(2)}) collective-permute-start(f32[256,512]{1,0:T(8,128)S(1)} %collective-permute-done.2.refs_2_.refs_12_), channel_id=1, source_target_pairs={{0,1},{1,0},{2,3},{3,2},{4,5},{5,4},{6,7},{7,6},{8,9},{9,8},{10,11... | collective-permute-start | bytes 1572872 | tf_op jit(solution)/shard_map/ppermute | solution.py:322
  31.2 0.0 collective-permute-done.refs_2_.refs_14_
  31.2 0.0 copy-start
  31.2 0.1 collective-permute-start.1
  31.3 0.7 pad_add_fusion.meta_ref
  32.0 3.4 %owned.1.refs_7_ = s32[2176]{0:T(1024)} custom-call(s32[3]{0:T(128)} %pad_add_fusion.meta_ref, s32[16,128]{1,0:T(8,128)} %bitcast.15), custom_call_target="tpu_custom_call" | custom-call | tf_op jit(solution)/shard_map/owned/pallas_call | solution.py:70
  35.4 14.0 %shard_map.46 = (f32[8,2,256]{2,1,0:T(2,128)}, bf16[4096,512]{1,0:T(8,128)(2,1)}, bf16[4096,512]{1,0:T(8,128)(2,1)}) custom-call(s32[3]{0:T(128)} %pad_add_fusion.meta_ref, s32[8,1,256]{2,1,0:T(1,128)} %bitcast.16, f32[8,1,256]{2,1,0:T(1,128)} %bitcast.19, f32[512,512]{1,0:T(8,128)} %refs_11_.1, f32[4096,512]{1,0:T(8,128)} %refs_10_.1), custom_call_target="tpu_custom_call" | custom-call | tf_op jit(solution)/shard_map/pallas_call | solution.py:302
  49.5 0.0 copy-done.2
  49.5 0.0 copy-done.3
  49.5 0.0 copy-done
  49.5 0.0 collective-permute-done.5.refs_5_.refs_17_
  49.5 0.0 copy-start.4
  49.5 0.0 collective-permute-done.3.refs_3_.refs_13_
  49.5 0.0 copy-start.5
  49.5 0.8 copy-done.4
  50.3 0.2 copy-done.5
  50.5 20.3 %shard_map.47.refs_6_ = f32[8,2,256]{2,1,0:T(2,128)} custom-call(s32[3]{0:T(128)} %pad_add_fusion.meta_ref, s32[8,1,256]{2,1,0:T(1,128)} %bitcast.17, f32[8,1,256]{2,1,0:T(1,128)} %bitcast.20, f32[256,512]{1,0:T(8,128)} %copy-done.3, f32[256,512]{1,0:T(8,128)} %copy-done.5, f32[256,512]{1,0:T(8,128)} %copy-done.2, f32[256,512]{1,0:T(8,128)} %copy-done.4, ...), custom_call_target="tpu_custom_call" | custom-call | tf_op jit(solution)/shard_map/pallas_call | solution.py:302
  70.8 0.0 collective-permute-done.1.refs_3_.refs_15_
  70.8 0.0 copy-start.1
  70.8 0.8 copy-done.1
  71.6 14.4 %shard_map.48 = f32[8,2,256]{2,1,0:T(2,128)} custom-call(s32[3]{0:T(128)} %pad_add_fusion.meta_ref, s32[8,1,256]{2,1,0:T(1,128)} %bitcast.18, f32[8,1,256]{2,1,0:T(1,128)} %bitcast.21, f32[256,512]{1,0:T(8,128)} %copy-done, f32[256,512]{1,0:T(8,128)} %copy-done.1, bf16[4096,512]{1,0:T(8,128)(2,1)} %get-tuple-element.8.refs_6_.refs_4_, ...), custom_call_target="tpu_custom_call" | custom-call | tf_op jit(solution)/shard_map/pallas_call | solution.py:302
  86.0 0.7 copy.10
  86.8 0.2 reshape.20
  86.9 0.1 copy.11
  87.0 0.1 all_to_all.8
  87.1 0.1 copy.12
  87.2 24.0 %all_to_all.12 = f32[256,1,16]{2,1,0:T(1,128)S(1)} all-to-all(f32[256,1,16]{2,1,0:T(1,128)S(1)} %copy.12), channel_id=1, replica_groups=mesh['dp'=4,'cls_0'=8,'cls_1'=4,'cls_2'=2] {'dp','cls_0','cls_1','cls_2'}, dimensions={0} | all-to-all | bytes 32768 | tf_op jit(solution)/shard_map/all_to_all | solution.py:343
  111.3 0.1 copy.13
  111.3 0.1 slice_reduce_fusion.1
  111.5 0.2 exponential_reduce_fusion
  111.6 0.5 add_subtract_fusion
Async XLA Ops:
  1.1 16.9 %collective-permute-start.4 = (f32[256,512]{1,0:T(8,128)S(1)}, f32[256,512]{1,0:T(8,128)S(1)}, u32[]{:S(2)}, u32[]{:S(2)}) collective-permute-start(f32[256,512]{1,0:T(8,128)S(1)} %constant_dynamic-slice_fusion), channel_id=1, source_target_pairs={{0,192},{64,0},{128,64},{192,128},{1,193},{65,1},{129,65},{193,129... | collective-permute-start | bytes 1572872 | tf_op jit(solution)/shard_map/ppermute | solution.py:323
  4.5 23.4 %collective-permute-start.2 = (f32[256,512]{1,0:T(8,128)S(1)}, f32[256,512]{1,0:T(8,128)S(1)}, u32[]{:S(2)}, u32[]{:S(2)}) collective-permute-start(f32[256,512]{1,0:T(8,128)S(1)} %constant_dynamic-slice_fusion), channel_id=1, source_target_pairs={{0,64},{64,128},{128,192},{192,0},{1,65},{65,129},{129,193},{193,1... | collective-permute-start | bytes 1572872 | tf_op jit(solution)/shard_map/ppermute | solution.py:323
  4.5 26.8 %collective-permute-start = (f32[256,512]{1,0:T(8,128)S(1)}, f32[256,512]{1,0:T(8,128)S(1)}, u32[]{:S(2)}, u32[]{:S(2)}) collective-permute-start(f32[256,512]{1,0:T(8,128)S(1)} %constant_dynamic-slice_fusion), channel_id=1, source_target_pairs={{0,128},{64,192},{128,0},{192,64},{1,129},{65,193},{129,1},{193,65... | collective-permute-start | bytes 1572872 | tf_op jit(solution)/shard_map/ppermute | solution.py:323
  18.0 31.5 %copy-start.2 = (f32[256,512]{1,0:T(8,128)}, f32[256,512]{1,0:T(8,128)S(1)}, u32[]{:S(2)}) copy-start(f32[256,512]{1,0:T(8,128)S(1)} %collective-permute-done.4.refs_4_.refs_16_) | copy-start | bytes 1572868
  18.0 31.5 %collective-permute-start.5 = (f32[256,512]{1,0:T(8,128)S(1)}, f32[256,512]{1,0:T(8,128)S(1)}, u32[]{:S(2)}, u32[]{:S(2)}) collective-permute-start(f32[256,512]{1,0:T(8,128)S(1)} %collective-permute-done.4.refs_4_.refs_16_), channel_id=1, source_target_pairs={{0,1},{1,0},{2,3},{3,2},{4,5},{5,4},{6,7},{7,6},{8,9},{9,8},{10,11... | collective-permute-start | bytes 1572872 | tf_op jit(solution)/shard_map/ppermute | solution.py:322
  27.8 21.7 %copy-start.3 = (f32[256,512]{1,0:T(8,128)}, f32[256,512]{1,0:T(8,128)S(1)}, u32[]{:S(2)}) copy-start(f32[256,512]{1,0:T(8,128)S(1)} %collective-permute-done.2.refs_2_.refs_12_) | copy-start | bytes 1572868
  27.8 21.7 %collective-permute-start.3 = (f32[256,512]{1,0:T(8,128)S(1)}, f32[256,512]{1,0:T(8,128)S(1)}, u32[]{:S(2)}, u32[]{:S(2)}) collective-permute-start(f32[256,512]{1,0:T(8,128)S(1)} %collective-permute-done.2.refs_2_.refs_12_), channel_id=1, source_target_pairs={{0,1},{1,0},{2,3},{3,2},{4,5},{5,4},{6,7},{7,6},{8,9},{9,8},{10,11... | collective-permute-start | bytes 1572872 | tf_op jit(solution)/shard_map/ppermute | solution.py:322
  31.2 18.2 %copy-start = (f32[256,512]{1,0:T(8,128)}, f32[256,512]{1,0:T(8,128)S(1)}, u32[]{:S(2)}) copy-start(f32[256,512]{1,0:T(8,128)S(1)} %collective-permute-done.refs_2_.refs_14_) | copy-start | bytes 1572868
  31.2 39.5 %collective-permute-start.1 = (f32[256,512]{1,0:T(8,128)S(1)}, f32[256,512]{1,0:T(8,128)S(1)}, u32[]{:S(2)}, u32[]{:S(2)}) collective-permute-start(f32[256,512]{1,0:T(8,128)S(1)} %collective-permute-done.refs_2_.refs_14_), channel_id=1, source_target_pairs={{0,1},{1,0},{2,3},{3,2},{4,5},{5,4},{6,7},{7,6},{8,9},{9,8},{10,11... | collective-permute-start | bytes 1572872 | tf_op jit(solution)/shard_map/ppermute | solution.py:322
  49.5 0.8 copy-start.4
  49.5 1.0 copy-start.5
  70.8 0.8 copy-start.1

commit v3 on v2

--- a/solution.py
+++ b/solution.py
@@ -74,6 +74,31 @@
         out_shape=jax.ShapeDtypeStruct((count + 128,), jnp.int32),
         name="owned",
     )(meta, labels.reshape(-1, 128))
+
+
+def scaled_kernel(meta_ref, values_ref, scales_ref, scaled_ref, mine_ref):
+    for h in range(2):
+        at = slice(h * HALF, (h + 1) * HALF)
+        values = values_ref[at, :]
+        inverse = lax.rsqrt(jnp.sum(values * values, axis=1, keepdims=True) + EPS)
+        scale = jnp.broadcast_to(scales_ref[2 * meta_ref[0] + h] * LOG2E, (8, HALF)).T[:, :1]
+        scaled_ref[at, :] = values * (inverse * scale)
+    mine_ref[...] = scaled_ref[pl.ds(pl.multiple_of(meta_ref[1] * HALF, HALF), HALF), :]
+
+
+def scaled_units(meta, embeddings, scales):
+    near = pl.BlockSpec(memory_space=pltpu.VMEM)
+    lines, width = embeddings.shape
+    return pl.pallas_call(
+        scaled_kernel,
+        in_specs=[pl.BlockSpec(memory_space=pltpu.SMEM), near, near],
+        out_specs=[near, near],
+        out_shape=[
+            jax.ShapeDtypeStruct((lines, width), jnp.float32),
+            jax.ShapeDtypeStruct((HALF, width), jnp.float32),
+        ],
+        name="scaled_units",
+    )(meta, embeddings, scales)
 
 
 def half_ids(meta_ref, shift, ways):
@@ -104,7 +129,7 @@
 def stats_kernel(meta_ref, *refs, shifts, ways, first, last):
     refs = list(refs)
     take = lambda n: [refs.pop(0) for _ in range(n)]
-    labels_ref, scales_ref = take(2)
+    (labels_ref,) = take(1)
     halves = take(len(shifts) if first else 2 * len(shifts))
     if first:
         (rows_ref,) = take(1)
@@ -155,11 +180,11 @@
                     slot = first_slot + k
                     number = jnp.where(slot < here, list_ref[base + slot], 0)
                     local = jnp.maximum(flat_labels_ref[number] - offset, 0)
-                    group_ref[0, k : k + 1, :] = found_ref[slot, pl.ds(lax.rem(number, 8), 1), :]
+                    scaled = found_ref[slot, pl.ds(lax.rem(number, 8), 1), :]
+                    group_ref[0, k : k + 1, :] = scaled / (flat_scales_ref[number] * LOG2E)
                     group_ref[1, k : k + 1, :] = picked_ref[slot, pl.ds(lax.rem(local, 8), 1), :]
                     numbers.append(number)
                 units, picked = group_ref[0], group_ref[1]
-                units = units * lax.rsqrt(jnp.sum(units * units, axis=1, keepdims=True) + EPS)
                 picked = picked * lax.rsqrt(jnp.sum(picked * picked, axis=1, keepdims=True) + EPS)
                 cosine = jnp.sum(units * picked, axis=1, keepdims=True)
                 across = units - cosine * picked
@@ -197,10 +222,7 @@
             if h < len(loads):
                 loads[h].wait()
             at = slice(h * HALF, (h + 1) * HALF)
-            values = raw_ref[at, :]
-            inverse = lax.rsqrt(jnp.sum(values * values, axis=1, keepdims=True) + EPS)
-            scale = jnp.broadcast_to(scales_ref[ids[h]] * LOG2E, (8, HALF)).T[:, :1]
-            high, low = split(values * (inverse * scale))
+            high, low = split(raw_ref[at, :])
             uh_ref[at, :] = high
             ul_ref[at, :] = low
             local_ref[:, at] = labels_ref[ids[h]] - offset
@@ -262,7 +284,7 @@
             lax.fori_loop(1, (found + SLOTS - 1) // SLOTS, batch, 0)
 
 
-def stats(meta, labels, scales, shifts, halves, rows, ways, before=None, extra=None):
+def stats(meta, labels, shifts, halves, rows, ways, before=None, extra=None):
     first, last = before is None, extra is not None
     rows_here, width = rows[0].shape
     blocks = labels.shape[0]
@@ -271,8 +293,8 @@
     far = pl.BlockSpec(memory_space=pl.ANY)
     scalars = pl.BlockSpec(memory_space=pltpu.SMEM)
     tiles = pl.BlockSpec((TILE, width), lambda t, meta: (t, 0))
-    in_specs = [whole(blocks, 1, HALF), whole(blocks, 1, HALF)] + [far] * len(halves) + [tiles] * len(rows)
-    args = [labels, scales, *halves, *rows]
+    in_specs = [whole(blocks, 1, HALF)] + [far] * len(halves) + [tiles] * len(rows)
+    args = [labels, *halves, *rows]
     out_specs = [whole(blocks, 2, HALF)]
     out_shape = [jax.ShapeDtypeStruct((blocks, 2, HALF), jnp.float32)]
     scratch = [
@@ -324,18 +346,19 @@
 
     label_blocks = labels.reshape(-1, 1, HALF)
     scale_blocks = row_scale.reshape(-1, 1, HALF)
-    mine = lax.dynamic_slice_in_dim(embeddings, core * HALF, HALF, 0)
+    scaled, mine = scaled_units(meta, embeddings, scale_blocks)
     left = shift(mine, 1)
     right = shift(mine, 3)
     across = shift(mine, 2)
     numbers = owned(meta, labels, rows_here)
-    held, high, low = stats(meta, label_blocks, scale_blocks, (0,), (embeddings,), (classifier,), ways)
+    held, high, low = stats(meta, label_blocks, (0,), (scaled,), (classifier,), ways)
     left_other = swap(left)
     near = (left, left_other, right, swap(right))
-    (held,) = stats(meta, label_blocks, scale_blocks, (1, 3), near, (high, low), ways, held)
-    far = (across, swap(across))
-    extra = [numbers, labels, row_scale, classifier, embeddings, near[0], near[1], *far, near[2], near[3]]
-    (held,) = stats(meta, label_blocks, scale_blocks, (2,), far, (high, low), ways, held, extra)
+    (held,) = stats(meta, label_blocks, (1, 3), near, (high, low), ways, held)
+    across_other = swap(across)
+    far = (across, across_other)
+    extra = [numbers, labels, row_scale, classifier, scaled, near[0], near[1], *far, near[2], near[3]]
+    (held,) = stats(meta, label_blocks, (2,), far, (high, low), ways, held, extra)
 
     devices = lax.axis_size(DP_CLS)
     share = count // devices

time: 113 us -> 113 us (level)
  Pallas kernels: 52.1 us -> 53.4 us
    pallas_call x0 -> x1, Pallas kernels: none -> 2.76 us  [scaled_units(): pl.pallas_call(scaled_kernel, in_specs=[pl.BlockSpec(memory_space=pltpu.S...]
    pallas_call x3, Pallas kernels: 48.7 us -> 47.2 us  [stats(): pl.pallas_call(functools.partial(stats_kernel, shifts=shifts, ways=ways,...]
  transfers between devices with their start and end apart: 6 -> 6, of which waited for: 1 -> 1; matrix products, arithmetic and copies ran while one was open for 1% -> 0% of each run, Pallas kernels for 34% -> 33%
where the time goes in v3:
time: 113 us
  Pallas kernels  53.4 us (47%)
  blocking collectives  24 us (21%)
  starting transfers between devices  18.2 us (16%)
  waiting for transfers between devices  12.2 us (11%)
  local copies, waits for them, and re-layouts  3.03 us (3%)
  other arithmetic  1.46 us (1%)
    pallas_call x3, Pallas kernels, stats(): pl.pallas_call(functools.partial(stats_kernel, shifts=shifts, ways=ways,...  47.2 us
    all_to_all x1, blocking collectives, body(): got = lax.all_to_all(send, DP_CLS, 0, 0, tiled=True)  24 us
    ppermute x3, starting transfers between devices, body(): swap = lambda part: lax.ppermute(part, 'cls_2', [(0, 1), (1, 0)])  13.2 us
    ppermute x3, waiting for transfers between devices, body(): lax.ppermute(part, 'dp', [(i, (i + k) % ways) for i in range(ways)])  12.2 us
    ppermute x3, starting transfers between devices, body(): lax.ppermute(part, 'dp', [(i, (i + k) % ways) for i in range(ways)])  5.03 us
    pallas_call x1, Pallas kernels, owned(): pl.pallas_call(functools.partial(owned_kernel, rows_here=rows_here), in_s...  3.45 us
    pallas_call x1, Pallas kernels, scaled_units(): pl.pallas_call(scaled_kernel, in_specs=[pl.BlockSpec(memory_space=pltpu.S...  2.76 us
  transfers between devices with their start and end apart: 6, of which 1 were waited for; matrix products, arithmetic and copies ran while one was open for 0% of the time, Pallas kernels for 33%

profile of v3, /device:TPU:1, one launch (start us, length us, event | category | flops | bytes accessed | tf_op | source)
XLA Modules:
  0.0 112.5 jit_solution(1710471469030058001)
XLA Ops:
  0.0 0.6 pad_add_fusion.meta_ref
  0.6 2.8 %scaled_units.1 = (f32[512,512]{1,0:T(8,128)}, f32[256,512]{1,0:T(8,128)}) custom-call(s32[3]{0:T(128)} %pad_add_fusion.meta_ref, f32[512,512]{1,0:T(8,128)} %values_ref.1, f32[8,1,256]{2,1,0:T(1,128)} %bitcast.21), custom_call_target="tpu_custom_call" | custom-call | tf_op jit(solution)/shard_map/scaled_units/pallas_call | solution.py:92
  3.4 3.3 %collective-permute-start.4 = (f32[256,512]{1,0:T(8,128)}, f32[256,512]{1,0:T(8,128)S(1)}, u32[]{:S(2)}, u32[]{:S(2)}) collective-permute-start(f32[256,512]{1,0:T(8,128)} %get-tuple-element.10), channel_id=1, source_target_pairs={{0,192},{64,0},{128,64},{192,128},{1,193},{65,1},{129,65},{193,129... | collective-permute-start | bytes 1572872 | tf_op jit(solution)/shard_map/ppermute | solution.py:345
  6.7 0.0 collective-permute-start.2
  6.7 1.7 %collective-permute-start = (f32[256,512]{1,0:T(8,128)}, f32[256,512]{1,0:T(8,128)S(1)}, u32[]{:S(2)}, u32[]{:S(2)}) collective-permute-start(f32[256,512]{1,0:T(8,128)} %get-tuple-element.10), channel_id=1, source_target_pairs={{0,128},{64,192},{128,0},{192,64},{1,129},{65,193},{129,1},{193,65... | collective-permute-start | bytes 1572872 | tf_op jit(solution)/shard_map/ppermute | solution.py:345
  8.4 12.2 %collective-permute-done.4.refs_3_.refs_15_ = f32[256,512]{1,0:T(8,128)S(1)} collective-permute-done((f32[256,512]{1,0:T(8,128)}, f32[256,512]{1,0:T(8,128)S(1)}, u32[]{:S(2)}, u32[]{:S(2)}) %collective-permute-start.4) | collective-permute-done | bytes 524320 | tf_op jit(solution)/shard_map/ppermute | solution.py:345
  20.6 0.0 copy-start
  20.6 9.8 %collective-permute-start.5 = (f32[256,512]{1,0:T(8,128)S(1)}, f32[256,512]{1,0:T(8,128)S(1)}, u32[]{:S(2)}, u32[]{:S(2)}) collective-permute-start(f32[256,512]{1,0:T(8,128)S(1)} %collective-permute-done.4.refs_3_.refs_15_), channel_id=1, source_target_pairs={{0,1},{1,0},{2,3},{3,2},{4,5},{5,4},{6,7},{7,6},{8,9},{9,8},{10,11... | collective-permute-start | bytes 1572872 | tf_op jit(solution)/shard_map/ppermute | solution.py:344
  30.4 0.0 collective-permute-done.2.refs_1_.refs_11_
  30.4 0.0 copy-start.1
  30.4 3.3 %collective-permute-start.3 = (f32[256,512]{1,0:T(8,128)S(1)}, f32[256,512]{1,0:T(8,128)S(1)}, u32[]{:S(2)}, u32[]{:S(2)}) collective-permute-start(f32[256,512]{1,0:T(8,128)S(1)} %collective-permute-done.2.refs_1_.refs_11_), channel_id=1, source_target_pairs={{0,1},{1,0},{2,3},{3,2},{4,5},{5,4},{6,7},{7,6},{8,9},{9,8},{10,11... | collective-permute-start | bytes 1572872 | tf_op jit(solution)/shard_map/ppermute | solution.py:344
  33.7 0.0 collective-permute-done.refs_1_.refs_13_
  33.7 0.0 copy-start.4
  33.7 0.1 collective-permute-start.1
  33.8 3.4 %owned.1.refs_6_ = s32[2176]{0:T(1024)} custom-call(s32[3]{0:T(128)} %pad_add_fusion.meta_ref, s32[16,128]{1,0:T(8,128)} %bitcast.15), custom_call_target="tpu_custom_call" | custom-call | tf_op jit(solution)/shard_map/owned/pallas_call | solution.py:70
  37.2 13.7 %shard_map.46 = (f32[8,2,256]{2,1,0:T(2,128)}, bf16[4096,512]{1,0:T(8,128)(2,1)}, bf16[4096,512]{1,0:T(8,128)(2,1)}) custom-call(s32[3]{0:T(128)} %pad_add_fusion.meta_ref, s32[8,1,256]{2,1,0:T(1,128)} %bitcast.16, f32[512,512]{1,0:T(8,128)} %get-tuple-element.11.refs_1_.refs_10_, f32[4096,512]{1,0:T(8,128)} %refs_9_.1), custom_call_target="tpu_custom_call" | custom-call | tf_op jit(solution)/shard_map/pallas_call | solution.py:324
  51.0 0.0 copy-done
  51.0 0.0 copy-done.1
  51.0 0.0 copy-done.4
  51.0 0.0 collective-permute-done.5.refs_4_.refs_16_
  51.0 0.0 copy-start.2
  51.0 0.0 collective-permute-done.3.refs_2_.refs_12_
  51.0 0.0 copy-start.3
  51.0 0.7 copy-done.2
  51.8 0.2 copy-done.3
  52.0 19.6 %shard_map.47.refs_5_ = f32[8,2,256]{2,1,0:T(2,128)} custom-call(s32[3]{0:T(128)} %pad_add_fusion.meta_ref, s32[8,1,256]{2,1,0:T(1,128)} %bitcast.17, f32[256,512]{1,0:T(8,128)} %copy-done.1, f32[256,512]{1,0:T(8,128)} %copy-done.3, f32[256,512]{1,0:T(8,128)} %copy-done, f32[256,512]{1,0:T(8,128)} %copy-done.2, ...), custom_call_target="tpu_custom_call" | custom-call | tf_op jit(solution)/shard_map/pallas_call | solution.py:324
  71.5 0.0 collective-permute-done.1.refs_2_.refs_14_
  71.6 0.0 copy-start.5
  71.6 0.8 copy-done.5
  72.4 14.0 %shard_map.48 = f32[8,2,256]{2,1,0:T(2,128)} custom-call(s32[3]{0:T(128)} %pad_add_fusion.meta_ref, s32[8,1,256]{2,1,0:T(1,128)} %bitcast.18, f32[256,512]{1,0:T(8,128)} %copy-done.4, f32[256,512]{1,0:T(8,128)} %copy-done.5, bf16[4096,512]{1,0:T(8,128)(2,1)} %get-tuple-element.12.refs_5_.refs_3_, bf16[4096,512]{1,0:T(8,128)(2,1)} %get-tuple-element.13.refs_6_.refs_4_, ...), custom_call_target="tpu_custom_call" | custom-call | tf_op jit(solution)/shard_map/pallas_call | solution.py:324
  86.3 0.7 copy.10
  87.1 0.2 reshape.20
  87.2 0.1 copy.11
  87.3 0.1 all_to_all.8
  87.4 0.1 copy.12
  87.5 24.0 %all_to_all.12 = f32[256,1,16]{2,1,0:T(1,128)S(1)} all-to-all(f32[256,1,16]{2,1,0:T(1,128)S(1)} %copy.12), channel_id=1, replica_groups=mesh['dp'=4,'cls_0'=8,'cls_1'=4,'cls_2'=2] {'dp','cls_0','cls_1','cls_2'}, dimensions={0} | all-to-all | bytes 32768 | tf_op jit(solution)/shard_map/all_to_all | solution.py:366
  111.6 0.1 copy.13
  111.6 0.1 slice_reduce_fusion.1
  111.8 0.2 exponential_reduce_fusion
  112.0 0.5 add_subtract_fusion
Async XLA Ops:
  3.4 17.2 %collective-permute-start.4 = (f32[256,512]{1,0:T(8,128)}, f32[256,512]{1,0:T(8,128)S(1)}, u32[]{:S(2)}, u32[]{:S(2)}) collective-permute-start(f32[256,512]{1,0:T(8,128)} %get-tuple-element.10), channel_id=1, source_target_pairs={{0,192},{64,0},{128,64},{192,128},{1,193},{65,1},{129,65},{193,129... | collective-permute-start | bytes 1572872 | tf_op jit(solution)/shard_map/ppermute | solution.py:345
  6.7 23.7 %collective-permute-start.2 = (f32[256,512]{1,0:T(8,128)}, f32[256,512]{1,0:T(8,128)S(1)}, u32[]{:S(2)}, u32[]{:S(2)}) collective-permute-start(f32[256,512]{1,0:T(8,128)} %get-tuple-element.10), channel_id=1, source_target_pairs={{0,64},{64,128},{128,192},{192,0},{1,65},{65,129},{129,193},{193,1... | collective-permute-start | bytes 1572872 | tf_op jit(solution)/shard_map/ppermute | solution.py:345
  6.7 27.0 %collective-permute-start = (f32[256,512]{1,0:T(8,128)}, f32[256,512]{1,0:T(8,128)S(1)}, u32[]{:S(2)}, u32[]{:S(2)}) collective-permute-start(f32[256,512]{1,0:T(8,128)} %get-tuple-element.10), channel_id=1, source_target_pairs={{0,128},{64,192},{128,0},{192,64},{1,129},{65,193},{129,1},{193,65... | collective-permute-start | bytes 1572872 | tf_op jit(solution)/shard_map/ppermute | solution.py:345
  20.6 30.4 %copy-start = (f32[256,512]{1,0:T(8,128)}, f32[256,512]{1,0:T(8,128)S(1)}, u32[]{:S(2)}) copy-start(f32[256,512]{1,0:T(8,128)S(1)} %collective-permute-done.4.refs_3_.refs_15_) | copy-start | bytes 1572868
  20.6 30.4 %collective-permute-start.5 = (f32[256,512]{1,0:T(8,128)S(1)}, f32[256,512]{1,0:T(8,128)S(1)}, u32[]{:S(2)}, u32[]{:S(2)}) collective-permute-start(f32[256,512]{1,0:T(8,128)S(1)} %collective-permute-done.4.refs_3_.refs_15_), channel_id=1, source_target_pairs={{0,1},{1,0},{2,3},{3,2},{4,5},{5,4},{6,7},{7,6},{8,9},{9,8},{10,11... | collective-permute-start | bytes 1572872 | tf_op jit(solution)/shard_map/ppermute | solution.py:344
  30.4 20.6 %copy-start.1 = (f32[256,512]{1,0:T(8,128)}, f32[256,512]{1,0:T(8,128)S(1)}, u32[]{:S(2)}) copy-start(f32[256,512]{1,0:T(8,128)S(1)} %collective-permute-done.2.refs_1_.refs_11_) | copy-start | bytes 1572868
  30.4 20.6 %collective-permute-start.3 = (f32[256,512]{1,0:T(8,128)S(1)}, f32[256,512]{1,0:T(8,128)S(1)}, u32[]{:S(2)}, u32[]{:S(2)}) collective-permute-start(f32[256,512]{1,0:T(8,128)S(1)} %collective-permute-done.2.refs_1_.refs_11_), channel_id=1, source_target_pairs={{0,1},{1,0},{2,3},{3,2},{4,5},{5,4},{6,7},{7,6},{8,9},{9,8},{10,11... | collective-permute-start | bytes 1572872 | tf_op jit(solution)/shard_map/ppermute | solution.py:344
  33.7 17.3 %copy-start.4 = (f32[256,512]{1,0:T(8,128)}, f32[256,512]{1,0:T(8,128)S(1)}, u32[]{:S(2)}) copy-start(f32[256,512]{1,0:T(8,128)S(1)} %collective-permute-done.refs_1_.refs_13_) | copy-start | bytes 1572868
  33.7 37.9 %collective-permute-start.1 = (f32[256,512]{1,0:T(8,128)S(1)}, f32[256,512]{1,0:T(8,128)S(1)}, u32[]{:S(2)}, u32[]{:S(2)}) collective-permute-start(f32[256,512]{1,0:T(8,128)S(1)} %collective-permute-done.refs_1_.refs_13_), channel_id=1, source_target_pairs={{0,1},{1,0},{2,3},{3,2},{4,5},{5,4},{6,7},{7,6},{8,9},{9,8},{10,11... | collective-permute-start | bytes 1572872 | tf_op jit(solution)/shard_map/ppermute | solution.py:344
  51.0 0.8 copy-start.2
  51.0 1.0 copy-start.3
  71.6 0.8 copy-start.5
